TPU v7x, 32 devices: a whole 2x2x4 slice. The times are simulated.
32 devices in a mesh: db: 8 (over y, x, core), pb: 4 (over z).
Axes of the slice: x: 2, y: 2, z: 4, core: 2. Of those that a mesh axis runs over, the one named last changes fastest.
Arguments:
- query_maps: bfloat16 [32, 256, 256], P(('db', 'pb')), may hold values from -6 to 6
- database: bfloat16 [1024, 256, 256], P(('db', 'pb')), may hold values from -6 to 6
- shortlist: int32 [32, 128], P(('db', 'pb')), may hold values from 0 to 1023, as said below
- kernel_query: bfloat16 [3, 3], replicated, may hold values from -1.5 to 1.5
- kernel_db: bfloat16 [3, 3], replicated, may hold values from -1.5 to 1.5
Outputs:
- scores: float32 [32, 128], P(('db', 'pb'))
- top_scores: float32 [32, 100], P(('db', 'pb'))
Inputs may be any that keep to these rules, and one draw needn't show every extreme that they name: Within one query the ids are distinct. Among the 128 shortlist entries of the query held by device q (query q), at most 8 lie in any one shard of images (ids s * 32 to (s + 1) * 32 - 1), and some shard holds exactly 8 of them for every device.
All inputs are finite; a program needn't handle non-finite values.
Results may differ from a plain program's by a relative error of at most 0.0003.
Values may be sent and summed in bfloat16 or wider, within the bound.
A program may use at most 128 MiB of HBM per device.

v0:
```python
import math
import jax
import jax.numpy as jnp
from jax import lax
from jax.sharding import PartitionSpec as P

GRID = 16
TOPK = 100
epsilon = 1e-06
score_scale = 8.0


def unit_maps(maps):
    values = maps.astype(jnp.float32)
    squares = jnp.sum(values * values, axis=1, keepdims=True)
    return (values * lax.rsqrt(squares + epsilon)).astype(jnp.bfloat16)


def conv_matrix(kernel):
    cell_count = GRID * GRID
    cell_index = jnp.arange(cell_count)
    row_out = (cell_index // GRID)[:, None]
    col_out = (cell_index % GRID)[:, None]
    row_in = (cell_index // GRID)[None, :]
    col_in = (cell_index % GRID)[None, :]
    weights = kernel.astype(jnp.float32)
    matrix = jnp.zeros((cell_count, cell_count), jnp.float32)
    for i in range(3):
        for j in range(3):
            hit = (row_in == row_out + i - 1) & (col_in == col_out + j - 1)
            matrix = matrix + weights[i, j] * hit.astype(jnp.float32)
    return matrix.astype(jnp.bfloat16)


def finish_pairs(correlation, conv_query, conv_db):
    rectified = jnp.maximum(correlation, 0.0).astype(jnp.bfloat16)
    filtered = jnp.einsum("qa,nab->nqb", conv_query, rectified, preferred_element_type=jnp.float32)
    filtered = filtered + jnp.einsum(
        "nqa,ba->nqb", rectified, conv_db, preferred_element_type=jnp.float32
    )
    return score_scale * jnp.mean(jnp.max(filtered, axis=1), axis=-1)


def shard_scores(gathered, slots, db_unit, conv_query, conv_db):
    source_count, width = slots.shape
    per_query = gathered.shape[0] // source_count
    grouped = gathered.reshape(source_count, per_query, gathered.shape[1], gathered.shape[2])
    step_size = math.gcd(source_count, max(1, 32 // width))

    def score_block(start):
        slot_block = lax.dynamic_slice_in_dim(slots, start, step_size, 0)
        group_block = lax.dynamic_slice_in_dim(grouped, start, step_size, 0)
        images = db_unit[slot_block]
        correlation = jnp.einsum(
            "scq,skcd->skqd", group_block[:, 0], images, preferred_element_type=jnp.float32
        )
        correlation = correlation.reshape(
            step_size * width, correlation.shape[-2], correlation.shape[-1]
        )
        return finish_pairs(correlation, conv_query, conv_db)

    starts = jnp.arange(source_count // step_size, dtype=jnp.int32) * step_size
    return lax.map(score_block, starts).reshape(source_count, width)


def body(query_maps, database, shortlist, kernel_query, kernel_db):
    query_unit = unit_maps(query_maps)
    db_unit = unit_maps(database)
    conv_query = conv_matrix(kernel_query)
    conv_db = conv_matrix(kernel_db)
    db_count = lax.axis_size("db")
    pb_count = lax.axis_size("pb")
    shard_count = db_count * pb_count
    per_query = query_maps.shape[0]
    cand_count = shortlist.shape[1]
    image_count = database.shape[0]
    flat_ids = shortlist.reshape(-1)
    row_count = flat_ids.shape[0]
    capacity = 2 * row_count // shard_count
    shard_of = flat_ids // image_count
    slot_of = flat_ids % image_count
    one_hot = (shard_of[:, None] == jnp.arange(shard_count, dtype=jnp.int32)[None, :]).astype(
        jnp.int32
    )
    bucket_pos = jnp.sum(jnp.cumsum(one_hot, axis=0) * one_hot, axis=1) - 1
    row_ids = jnp.arange(row_count, dtype=jnp.int32)
    query_of = row_ids // cand_count
    empty = jnp.zeros((shard_count, capacity), jnp.int32)
    send_slot = empty.at[shard_of, bucket_pos].set(slot_of)
    send_query = empty.at[shard_of, bucket_pos].set(query_of)
    requests = jnp.stack([send_slot, send_query])
    gathered = lax.all_gather(query_unit, ("db", "pb"), axis=0, tiled=True)
    found = shard_scores(
        gathered,
        lax.all_to_all(requests, ("db", "pb"), split_axis=1, concat_axis=1, tiled=True)[0],
        db_unit,
        conv_query,
        conv_db,
    )
    returned = lax.all_to_all(found, ("db", "pb"), split_axis=0, concat_axis=0, tiled=True)
    scores = returned[shard_of, bucket_pos].reshape(per_query, cand_count)
    top_scores = lax.top_k(scores, TOPK)[0]
    return (scores, top_scores)


def solution(mesh):
    in_specs = (
        P(("db", "pb"), None, None),
        P(("db", "pb"), None, None),
        P(("db", "pb"), None),
        P(),
        P(),
    )
    out_specs = (P(("db", "pb"), None), P(("db", "pb"), None))
    return jax.shard_map(body, mesh=mesh, in_specs=in_specs, out_specs=out_specs, check_vma=False)
```

profile of v0, /device:TPU:0, one launch (start us, length us, event | category | flops | bytes accessed | tf_op | source)
XLA Modules:
  0.0 317.0 jit_solution(1332410492687568349)
XLA Ops:
  11.6 6.4 %scatter_fusion = s32[32,8]{0,1:T(8,128)S(1)} fusion(s32[32,8]{0,1:T(8,128)S(1)} %broadcast_in_dim.11.clone.1, s32[128]{0:T(128)S(1)} %fusion.60, s32[128]{0:T(128)S(1)} %get-tuple-element.427), kind=kCustom, calls=%fused_computation.2 | custom fusion | bytes 2560 | tf_op jit(solution)/shard_map/scatter | solution.py:89
  18.1 6.4 %scatter_fusion.1 = s32[32,8]{0,1:T(8,128)S(1)} fusion(s32[32,8]{0,1:T(8,128)S(1)} %broadcast_in_dim.11.clone, s32[128]{0:T(128)S(1)} %fusion.60, s32[128]{0:T(128)S(1)} %and_select_fusion.2), kind=kCustom, calls=%fused_computation.3 | custom fusion | bytes 2560 | tf_op jit(solution)/shard_map/scatter | solution.py:90
  25.2 7.3 %all-to-all-start = ((s32[2,32,8]{2,0,1:T(2,128)}), s32[2,32,8]{2,0,1:T(2,128)S(1)}, u32[]{:S(2)}, u32[]{:S(2)}) async-start(s32[2,32,8]{2,0,1:T(2,128)} %copy.23), calls=%async_computation | async-start | bytes 65536 | tf_op jit(solution)/shard_map/all_to_all | solution.py:95
  42.2 33.2 %all-gather.2.cloned.1.call-done = bf16[32,256,256]{2,1,0:T(8,128)(2,1)} async-done(((bf16[1,256,256]{2,1,0:T(8,128)(2,1)}), bf16[32,256,256]{2,1,0:T(8,128)(2,1)}) %all-gather.2.cloned.1.call-update) | async-done | bytes 4194320 | tf_op jit(solution)/shard_map/all_gather | solution.py:92
  75.4 220.3 %while.14 = (s32[]{:T(128)}, f32[8,32]{1,0:T(8,128)S(1)}, s32[8]{0:T(128)S(1)}, s32[32,8]{1,0:T(8,128)S(1)}, bf16[32,256,256]{2,1,0:T(8,128)(2,1)}, /*index=5*/b...) while((s32[]{:T(128)}, f32[8,32]{1,0:T(8,128)S(1)}, ...), condition=%wide.region_9.10_spmd.clone.clone, body=%wide.region_6.9_spmd.clone.clone.sunk | while | flops 3233940480 | bytes 42551080 | solution.py:63
  77.8 5.0 %gather_fusion = bf16[32,256,256]{2,1,0:T(8,128)(2,1)} fusion(bf16[32,256,256]{2,1,0:T(8,128)(2,1)} %get-tuple-element.688, s32[1024]{0:T(1024)S(1)} %pad_clamp_fusion.2), kind=kCustom, calls=%fused_computation.clone.clone.clone.1 | custom fusion | bytes 8388736 | tf_op jit(solution)/shard_map/while/body/eval_jaxpr/gather | solution.py:53
  86.8 7.3 %fusion.81 = f32[32,256,256]{1,2,0:T(8,128)S(1)} fusion(bf16[32,256,256]{1,2,0:T(8,128)(2,1)S(1)} %bitcast.124, f32[]{:T(128)} %get-tuple-element.704, f32[]{:T(128)} %get-tuple-element.701, f32[]{:T(128)} %get-tuple-element.699, f32[]{:T(128)} %get-tuple-element.697, f32[]{:T(128)} %get-tuple-element.695, f32[]{:T(128)} %get-tuple-element.694, ...), kind=kOutput, calls=%fused_computation.23.clone.1 | convolution fusion | flops 1075904512 | bytes 12589092 | tf_op jit(solution)/shard_map/while/body/eval_jaxpr/qa,nab->nqb/dot_general | solution.py:37
  94.1 8.6 %fusion.82 = f32[32,256]{1,0:T(8,128)S(1)} fusion(f32[32,256,256]{1,2,0:T(8,128)S(1)} %fusion.81, bf16[32,256,256]{1,2,0:T(8,128)(2,1)S(1)} %bitcast.125, f32[]{:T(128)} %get-tuple-element.713, f32[]{:T(128)} %get-tuple-element.712, f32[]{:T(128)} %get-tuple-element.711, f32[]{:T(128)} %get-tuple-element.710, f32[]{:T(128)} %get-tuple-element.709, ...), kind=kOutput, calls=%fused_computation.7.clone.1 | convolution fusion | flops 1080090624 | bytes 12621860 | tf_op jit(solution)/shard_map/while/body/eval_jaxpr/nqa,ba->nqb/dot_general | solution.py:38
  105.3 5.0 %gather_fusion = bf16[32,256,256]{2,1,0:T(8,128)(2,1)} fusion(bf16[32,256,256]{2,1,0:T(8,128)(2,1)} %get-tuple-element.688, s32[1024]{0:T(1024)S(1)} %pad_clamp_fusion.2), kind=kCustom, calls=%fused_computation.clone.clone.clone.1 | custom fusion | bytes 8388736 | tf_op jit(solution)/shard_map/while/body/eval_jaxpr/gather | solution.py:53
  114.3 7.3 %fusion.81 = f32[32,256,256]{1,2,0:T(8,128)S(1)} fusion(bf16[32,256,256]{1,2,0:T(8,128)(2,1)S(1)} %bitcast.124, f32[]{:T(128)} %get-tuple-element.704, f32[]{:T(128)} %get-tuple-element.701, f32[]{:T(128)} %get-tuple-element.699, f32[]{:T(128)} %get-tuple-element.697, f32[]{:T(128)} %get-tuple-element.695, f32[]{:T(128)} %get-tuple-element.694, ...), kind=kOutput, calls=%fused_computation.23.clone.1 | convolution fusion | flops 1075904512 | bytes 12589092 | tf_op jit(solution)/shard_map/while/body/eval_jaxpr/qa,nab->nqb/dot_general | solution.py:37
  121.6 8.6 %fusion.82 = f32[32,256]{1,0:T(8,128)S(1)} fusion(f32[32,256,256]{1,2,0:T(8,128)S(1)} %fusion.81, bf16[32,256,256]{1,2,0:T(8,128)(2,1)S(1)} %bitcast.125, f32[]{:T(128)} %get-tuple-element.713, f32[]{:T(128)} %get-tuple-element.712, f32[]{:T(128)} %get-tuple-element.711, f32[]{:T(128)} %get-tuple-element.710, f32[]{:T(128)} %get-tuple-element.709, ...), kind=kOutput, calls=%fused_computation.7.clone.1 | convolution fusion | flops 1080090624 | bytes 12621860 | tf_op jit(solution)/shard_map/while/body/eval_jaxpr/nqa,ba->nqb/dot_general | solution.py:38
  141.8 7.3 %fusion.81 = f32[32,256,256]{1,2,0:T(8,128)S(1)} fusion(bf16[32,256,256]{1,2,0:T(8,128)(2,1)S(1)} %bitcast.124, f32[]{:T(128)} %get-tuple-element.704, f32[]{:T(128)} %get-tuple-element.701, f32[]{:T(128)} %get-tuple-element.699, f32[]{:T(128)} %get-tuple-element.697, f32[]{:T(128)} %get-tuple-element.695, f32[]{:T(128)} %get-tuple-element.694, ...), kind=kOutput, calls=%fused_computation.23.clone.1 | convolution fusion | flops 1075904512 | bytes 12589092 | tf_op jit(solution)/shard_map/while/body/eval_jaxpr/qa,nab->nqb/dot_general | solution.py:37
  149.2 8.6 %fusion.82 = f32[32,256]{1,0:T(8,128)S(1)} fusion(f32[32,256,256]{1,2,0:T(8,128)S(1)} %fusion.81, bf16[32,256,256]{1,2,0:T(8,128)(2,1)S(1)} %bitcast.125, f32[]{:T(128)} %get-tuple-element.713, f32[]{:T(128)} %get-tuple-element.712, f32[]{:T(128)} %get-tuple-element.711, f32[]{:T(128)} %get-tuple-element.710, f32[]{:T(128)} %get-tuple-element.709, ...), kind=kOutput, calls=%fused_computation.7.clone.1 | convolution fusion | flops 1080090624 | bytes 12621860 | tf_op jit(solution)/shard_map/while/body/eval_jaxpr/nqa,ba->nqb/dot_general | solution.py:38
  169.4 7.3 %fusion.81 = f32[32,256,256]{1,2,0:T(8,128)S(1)} fusion(bf16[32,256,256]{1,2,0:T(8,128)(2,1)S(1)} %bitcast.124, f32[]{:T(128)} %get-tuple-element.704, f32[]{:T(128)} %get-tuple-element.701, f32[]{:T(128)} %get-tuple-element.699, f32[]{:T(128)} %get-tuple-element.697, f32[]{:T(128)} %get-tuple-element.695, f32[]{:T(128)} %get-tuple-element.694, ...), kind=kOutput, calls=%fused_computation.23.clone.1 | convolution fusion | flops 1075904512 | bytes 12589092 | tf_op jit(solution)/shard_map/while/body/eval_jaxpr/qa,nab->nqb/dot_general | solution.py:37
  176.7 8.6 %fusion.82 = f32[32,256]{1,0:T(8,128)S(1)} fusion(f32[32,256,256]{1,2,0:T(8,128)S(1)} %fusion.81, bf16[32,256,256]{1,2,0:T(8,128)(2,1)S(1)} %bitcast.125, f32[]{:T(128)} %get-tuple-element.713, f32[]{:T(128)} %get-tuple-element.712, f32[]{:T(128)} %get-tuple-element.711, f32[]{:T(128)} %get-tuple-element.710, f32[]{:T(128)} %get-tuple-element.709, ...), kind=kOutput, calls=%fused_computation.7.clone.1 | convolution fusion | flops 1080090624 | bytes 12621860 | tf_op jit(solution)/shard_map/while/body/eval_jaxpr/nqa,ba->nqb/dot_general | solution.py:38
  196.9 7.3 %fusion.81 = f32[32,256,256]{1,2,0:T(8,128)S(1)} fusion(bf16[32,256,256]{1,2,0:T(8,128)(2,1)S(1)} %bitcast.124, f32[]{:T(128)} %get-tuple-element.704, f32[]{:T(128)} %get-tuple-element.701, f32[]{:T(128)} %get-tuple-element.699, f32[]{:T(128)} %get-tuple-element.697, f32[]{:T(128)} %get-tuple-element.695, f32[]{:T(128)} %get-tuple-element.694, ...), kind=kOutput, calls=%fused_computation.23.clone.1 | convolution fusion | flops 1075904512 | bytes 12589092 | tf_op jit(solution)/shard_map/while/body/eval_jaxpr/qa,nab->nqb/dot_general | solution.py:37
  204.3 8.6 %fusion.82 = f32[32,256]{1,0:T(8,128)S(1)} fusion(f32[32,256,256]{1,2,0:T(8,128)S(1)} %fusion.81, bf16[32,256,256]{1,2,0:T(8,128)(2,1)S(1)} %bitcast.125, f32[]{:T(128)} %get-tuple-element.713, f32[]{:T(128)} %get-tuple-element.712, f32[]{:T(128)} %get-tuple-element.711, f32[]{:T(128)} %get-tuple-element.710, f32[]{:T(128)} %get-tuple-element.709, ...), kind=kOutput, calls=%fused_computation.7.clone.1 | convolution fusion | flops 1080090624 | bytes 12621860 | tf_op jit(solution)/shard_map/while/body/eval_jaxpr/nqa,ba->nqb/dot_general | solution.py:38
  224.5 7.3 %fusion.81 = f32[32,256,256]{1,2,0:T(8,128)S(1)} fusion(bf16[32,256,256]{1,2,0:T(8,128)(2,1)S(1)} %bitcast.124, f32[]{:T(128)} %get-tuple-element.704, f32[]{:T(128)} %get-tuple-element.701, f32[]{:T(128)} %get-tuple-element.699, f32[]{:T(128)} %get-tuple-element.697, f32[]{:T(128)} %get-tuple-element.695, f32[]{:T(128)} %get-tuple-element.694, ...), kind=kOutput, calls=%fused_computation.23.clone.1 | convolution fusion | flops 1075904512 | bytes 12589092 | tf_op jit(solution)/shard_map/while/body/eval_jaxpr/qa,nab->nqb/dot_general | solution.py:37
  231.8 8.6 %fusion.82 = f32[32,256]{1,0:T(8,128)S(1)} fusion(f32[32,256,256]{1,2,0:T(8,128)S(1)} %fusion.81, bf16[32,256,256]{1,2,0:T(8,128)(2,1)S(1)} %bitcast.125, f32[]{:T(128)} %get-tuple-element.713, f32[]{:T(128)} %get-tuple-element.712, f32[]{:T(128)} %get-tuple-element.711, f32[]{:T(128)} %get-tuple-element.710, f32[]{:T(128)} %get-tuple-element.709, ...), kind=kOutput, calls=%fused_computation.7.clone.1 | convolution fusion | flops 1080090624 | bytes 12621860 | tf_op jit(solution)/shard_map/while/body/eval_jaxpr/nqa,ba->nqb/dot_general | solution.py:38
  252.0 7.3 %fusion.81 = f32[32,256,256]{1,2,0:T(8,128)S(1)} fusion(bf16[32,256,256]{1,2,0:T(8,128)(2,1)S(1)} %bitcast.124, f32[]{:T(128)} %get-tuple-element.704, f32[]{:T(128)} %get-tuple-element.701, f32[]{:T(128)} %get-tuple-element.699, f32[]{:T(128)} %get-tuple-element.697, f32[]{:T(128)} %get-tuple-element.695, f32[]{:T(128)} %get-tuple-element.694, ...), kind=kOutput, calls=%fused_computation.23.clone.1 | convolution fusion | flops 1075904512 | bytes 12589092 | tf_op jit(solution)/shard_map/while/body/eval_jaxpr/qa,nab->nqb/dot_general | solution.py:37
  259.4 8.6 %fusion.82 = f32[32,256]{1,0:T(8,128)S(1)} fusion(f32[32,256,256]{1,2,0:T(8,128)S(1)} %fusion.81, bf16[32,256,256]{1,2,0:T(8,128)(2,1)S(1)} %bitcast.125, f32[]{:T(128)} %get-tuple-element.713, f32[]{:T(128)} %get-tuple-element.712, f32[]{:T(128)} %get-tuple-element.711, f32[]{:T(128)} %get-tuple-element.710, f32[]{:T(128)} %get-tuple-element.709, ...), kind=kOutput, calls=%fused_computation.7.clone.1 | convolution fusion | flops 1080090624 | bytes 12621860 | tf_op jit(solution)/shard_map/while/body/eval_jaxpr/nqa,ba->nqb/dot_general | solution.py:38
  279.6 7.3 %fusion.81 = f32[32,256,256]{1,2,0:T(8,128)S(1)} fusion(bf16[32,256,256]{1,2,0:T(8,128)(2,1)S(1)} %bitcast.124, f32[]{:T(128)} %get-tuple-element.704, f32[]{:T(128)} %get-tuple-element.701, f32[]{:T(128)} %get-tuple-element.699, f32[]{:T(128)} %get-tuple-element.697, f32[]{:T(128)} %get-tuple-element.695, f32[]{:T(128)} %get-tuple-element.694, ...), kind=kOutput, calls=%fused_computation.23.clone.1 | convolution fusion | flops 1075904512 | bytes 12589092 | tf_op jit(solution)/shard_map/while/body/eval_jaxpr/qa,nab->nqb/dot_general | solution.py:37
  286.9 8.6 %fusion.82 = f32[32,256]{1,0:T(8,128)S(1)} fusion(f32[32,256,256]{1,2,0:T(8,128)S(1)} %fusion.81, bf16[32,256,256]{1,2,0:T(8,128)(2,1)S(1)} %bitcast.125, f32[]{:T(128)} %get-tuple-element.713, f32[]{:T(128)} %get-tuple-element.712, f32[]{:T(128)} %get-tuple-element.711, f32[]{:T(128)} %get-tuple-element.710, f32[]{:T(128)} %get-tuple-element.709, ...), kind=kOutput, calls=%fused_computation.7.clone.1 | convolution fusion | flops 1080090624 | bytes 12621860 | tf_op jit(solution)/shard_map/while/body/eval_jaxpr/nqa,ba->nqb/dot_general | solution.py:38
  295.8 10.4 %all_to_all.17 = f32[32,1,8]{2,1,0:T(1,128)S(1)} all-to-all(f32[32,1,8]{2,1,0:T(1,128)S(1)} %bitcast.131), channel_id=1, replica_groups=mesh['db'=8,'pb'=4] {'db','pb'}, dimensions={0} | all-to-all | bytes 2048 | tf_op jit(solution)/shard_map/all_to_all | solution.py:100
  (106 shorter events, 87.2 us)
Async XLA Ops:
  7.2 68.2 %all-gather.2.cloned.1.call-start = ((), (), s32[]{:S(2)}) async-start(), calls=%async_computation.2 | async-start | bytes 4325376 | tf_op jit(solution)/shard_map/all_gather | solution.py:92
  25.2 16.9 %all-to-all-start = ((s32[2,32,8]{2,0,1:T(2,128)}), s32[2,32,8]{2,0,1:T(2,128)S(1)}, u32[]{:S(2)}, u32[]{:S(2)}) async-start(s32[2,32,8]{2,0,1:T(2,128)} %copy.23), calls=%async_computation | async-start | bytes 65536 | tf_op jit(solution)/shard_map/all_to_all | solution.py:95
  32.5 6.5 %copy-start = (bf16[32,256,256]{2,1,0:T(8,128)(2,1)S(1)}, bf16[32,256,256]{2,1,0:T(8,128)(2,1)}, u32[]{:S(2)}) copy-start(bf16[32,256,256]{2,1,0:T(8,128)(2,1)} %param.8) | copy-start | bytes 12582916
  307.5 2.7 copy-start.1
Sparse Core Ops, SparseCore 0:
  11.0 64.3 all-gather.1
where the time goes:
time: 319 us; the launch traced here: 317 us
  matrix products  160 us (50%)
  local copies, waits for them, and re-layouts  63.6 us (20%)
  waiting for transfers between devices  33.2 us (10%)
  other arithmetic  14.3 us (4%)
  between operations  14.2 us (4%)
  loops' own time  14 us (4%)
  blocking collectives  10.4 us (3%)
  starting transfers between devices  7.36 us (2%)
    dot_general x8, matrix products, finish_pairs(): jnp.einsum('nqa,ba->nqb', rectified, conv_db, preferred_element_type=jnp....  69.1 us
    dot_general x8, matrix products, finish_pairs(): jnp.einsum('qa,nab->nqb', conv_query, rectified, preferred_element_type=j...  58.8 us
    gather x8, local copies, waits for them, and re-layouts, score_block(): images = db_unit[slot_block]  39.8 us
    all_gather x1, waiting for transfers between devices, body(): gathered = lax.all_gather(query_unit, ('db', 'pb'), axis=0, tiled=True)  33.2 us
    dot_general x8, matrix products, score_block(): jnp.einsum('scq,skcd->skqd', group_block[:, 0], images, preferred_element...  32.1 us
    another operation x1, loops' own time, shard_scores(): return lax.map(score_block, starts).reshape(source_count, width)  14 us
    all_to_all x1, blocking collectives, body(): lax.all_to_all(found, ('db', 'pb'), split_axis=0, concat_axis=0, tiled=True)  10.4 us
    all_to_all x1, starting transfers between devices, body(): lax.all_to_all(requests, ('db', 'pb'), split_axis=1, concat_axis=1, tiled...  7.33 us
  transfers between devices with their start and end apart: 2, of which 1 were waited for; matrix products, arithmetic and copies ran while one was open for 8% of the time, Pallas kernels for 0%

commit v1 on v0

--- a/solution.py
+++ b/solution.py
@@ -89,7 +89,10 @@
     send_slot = empty.at[shard_of, bucket_pos].set(slot_of)
     send_query = empty.at[shard_of, bucket_pos].set(query_of)
     requests = jnp.stack([send_slot, send_query])
-    gathered = lax.all_gather(query_unit, ("db", "pb"), axis=0, tiled=True)
+    n_dev = lax.axis_size(("db", "pb"))
+    blocks = jnp.stack([query_unit for _ in range(n_dev)])
+    blocks = lax.all_to_all(blocks, ("db", "pb"), split_axis=0, concat_axis=0)
+    gathered = jnp.concatenate(blocks, axis=0)
     found = shard_scores(
         gathered,
         lax.all_to_all(requests, ("db", "pb"), split_axis=1, concat_axis=1, tiled=True)[0],

time: 319 us -> 368 us (1.15)
  waiting for transfers between devices: 33.2 us -> 90 us
  between operations: 14.2 us -> 0.83 us
    all_to_all x0 -> x1, waiting for transfers between devices: none -> 84.6 us  [body(): blocks = lax.all_to_all(blocks, ('db', 'pb'), split_axis=0, concat_axis=0)]
    all_gather x1 -> x0, waiting for transfers between devices: 33.2 us -> none  [body(): gathered = lax.all_gather(query_unit, ('db', 'pb'), axis=0, tiled=True)]
    all_to_all x1, waiting for transfers between devices: 0.01 us -> 5.4 us  [body(): lax.all_to_all(requests, ('db', 'pb'), split_axis=1, concat_axis=1, tiled...]
    all_to_all x0 -> x1, starting transfers between devices: none -> 3.7 us  [body(): blocks = lax.all_to_all(blocks, ('db', 'pb'), split_axis=0, concat_axis=0)]
  transfers between devices with their start and end apart: 2 -> 2, of which waited for: 1 -> 2; matrix products, arithmetic and copies ran while one was open for 8% -> 3% of each run, Pallas kernels for 0% -> 0%
where the time goes in v1:
time: 368 us; the launch traced here: 366 us
  matrix products  160 us (43%)
  waiting for transfers between devices  90 us (24%)
  local copies, waits for them, and re-layouts  64 us (17%)
  loops' own time  14 us (4%)
  other arithmetic  13.6 us (4%)
  blocking collectives  12.5 us (3%)
  starting transfers between devices  11 us (3%)
    all_to_all x1, waiting for transfers between devices, body(): blocks = lax.all_to_all(blocks, ('db', 'pb'), split_axis=0, concat_axis=0)  84.6 us
    dot_general x8, matrix products, finish_pairs(): jnp.einsum('nqa,ba->nqb', rectified, conv_db, preferred_element_type=jnp....  69 us
    dot_general x8, matrix products, finish_pairs(): jnp.einsum('qa,nab->nqb', conv_query, rectified, preferred_element_type=j...  58.7 us
    gather x8, local copies, waits for them, and re-layouts, score_block(): images = db_unit[slot_block]  39.8 us
    dot_general x8, matrix products, score_block(): jnp.einsum('scq,skcd->skqd', group_block[:, 0], images, preferred_element...  32.1 us
    another operation x1, loops' own time, shard_scores(): return lax.map(score_block, starts).reshape(source_count, width)  14 us
    all_to_all x1, blocking collectives, body(): lax.all_to_all(found, ('db', 'pb'), split_axis=0, concat_axis=0, tiled=True)  12.5 us
  transfers between devices with their start and end apart: 2, of which 2 were waited for; matrix products, arithmetic and copies ran while one was open for 3% of the time, Pallas kernels for 0%

profile of v1, /device:TPU:0, one launch (start us, length us, event | category | flops | bytes accessed | tf_op | source)
XLA Modules:
  0.0 365.8 jit_solution(1738204758392143371)
XLA Ops:
  2.5 6.4 %scatter_fusion = s32[32,8]{0,1:T(8,128)S(1)} fusion(s32[32,8]{0,1:T(8,128)S(1)} %broadcast_in_dim.11.clone.1, s32[128]{0:T(128)S(1)} %fusion.61, s32[128]{0:T(128)S(1)} %get-tuple-element.487), kind=kCustom, calls=%fused_computation.2 | custom fusion | bytes 2560 | tf_op jit(solution)/shard_map/scatter | solution.py:89
  8.9 6.4 %scatter_fusion.1 = s32[32,8]{0,1:T(8,128)S(1)} fusion(s32[32,8]{0,1:T(8,128)S(1)} %broadcast_in_dim.11.clone, s32[128]{0:T(128)S(1)} %fusion.61, s32[128]{0:T(128)S(1)} %and_select_fusion.2), kind=kCustom, calls=%fused_computation.3 | custom fusion | bytes 2560 | tf_op jit(solution)/shard_map/scatter | solution.py:90
  16.0 7.3 %all-to-all-start = ((s32[2,32,8]{2,0,1:T(2,128)}), s32[2,32,8]{2,0,1:T(2,128)S(1)}, u32[]{:S(2)}, u32[]{:S(2)}) async-start(s32[2,32,8]{2,0,1:T(2,128)} %copy.24), calls=%async_computation | async-start | bytes 65536 | tf_op jit(solution)/shard_map/all_to_all | solution.py:98
  25.3 5.4 %all-to-all-done = s32[2,32,8]{2,0,1:T(2,128)S(1)} async-done(((s32[2,32,8]{2,0,1:T(2,128)}), s32[2,32,8]{2,0,1:T(2,128)S(1)}, u32[]{:S(2)}, u32[]{:S(2)}) %all-to-all-start) | async-done | bytes 2080 | tf_op jit(solution)/shard_map/all_to_all | solution.py:98
  44.4 84.6 %all-to-all-done.1 = bf16[32,1,256,256]{3,2,1,0:T(8,128)(2,1)} async-done(((bf16[32,1,256,256]{3,2,1,0:T(8,128)(2,1)}), bf16[32,1,256,256]{3,2,1,0:T(8,128)(2,1)}, u32[]{:S(2)}, u32[]{:S(2)}) %all-to-all-start.1) | async-done | bytes 4194336 | tf_op jit(solution)/shard_map/all_to_all | solution.py:94
  129.0 220.2 %while.14 = (s32[]{:T(128)}, f32[8,32]{1,0:T(8,128)S(1)}, s32[8]{0:T(128)S(1)}, s32[32,8]{1,0:T(8,128)S(1)}, bf16[32,256,256]{2,1,0:T(8,128)(2,1)}, /*index=5*/b...) while((s32[]{:T(128)}, f32[8,32]{1,0:T(8,128)S(1)}, ...), condition=%wide.region_9.10_spmd.clone.clone, body=%wide.region_6.9_spmd.clone.clone.sunk | while | flops 3233940480 | bytes 42551080 | solution.py:63
  140.4 7.3 %fusion.82 = f32[32,256,256]{1,2,0:T(8,128)S(1)} fusion(bf16[32,256,256]{1,2,0:T(8,128)(2,1)S(1)} %bitcast.126, f32[]{:T(128)} %get-tuple-element.764, f32[]{:T(128)} %get-tuple-element.761, f32[]{:T(128)} %get-tuple-element.759, f32[]{:T(128)} %get-tuple-element.757, f32[]{:T(128)} %get-tuple-element.755, f32[]{:T(128)} %get-tuple-element.754, ...), kind=kOutput, calls=%fused_computation.23.clone.1 | convolution fusion | flops 1075904512 | bytes 12589092 | tf_op jit(solution)/shard_map/while/body/eval_jaxpr/qa,nab->nqb/dot_general | solution.py:37
  147.8 8.6 %fusion.83 = f32[32,256]{1,0:T(8,128)S(1)} fusion(f32[32,256,256]{1,2,0:T(8,128)S(1)} %fusion.82, bf16[32,256,256]{1,2,0:T(8,128)(2,1)S(1)} %bitcast.127, f32[]{:T(128)} %get-tuple-element.773, f32[]{:T(128)} %get-tuple-element.772, f32[]{:T(128)} %get-tuple-element.771, f32[]{:T(128)} %get-tuple-element.770, f32[]{:T(128)} %get-tuple-element.769, ...), kind=kOutput, calls=%fused_computation.7.clone.1 | convolution fusion | flops 1080090624 | bytes 12621860 | tf_op jit(solution)/shard_map/while/body/eval_jaxpr/nqa,ba->nqb/dot_general | solution.py:38
  158.9 5.0 %gather_fusion = bf16[32,256,256]{2,1,0:T(8,128)(2,1)} fusion(bf16[32,256,256]{2,1,0:T(8,128)(2,1)} %get-tuple-element.748, s32[1024]{0:T(1024)S(1)} %pad_clamp_fusion.2), kind=kCustom, calls=%fused_computation.clone.clone.clone.1 | custom fusion | bytes 8388736 | tf_op jit(solution)/shard_map/while/body/eval_jaxpr/gather | solution.py:53
  167.9 7.3 %fusion.82 = f32[32,256,256]{1,2,0:T(8,128)S(1)} fusion(bf16[32,256,256]{1,2,0:T(8,128)(2,1)S(1)} %bitcast.126, f32[]{:T(128)} %get-tuple-element.764, f32[]{:T(128)} %get-tuple-element.761, f32[]{:T(128)} %get-tuple-element.759, f32[]{:T(128)} %get-tuple-element.757, f32[]{:T(128)} %get-tuple-element.755, f32[]{:T(128)} %get-tuple-element.754, ...), kind=kOutput, calls=%fused_computation.23.clone.1 | convolution fusion | flops 1075904512 | bytes 12589092 | tf_op jit(solution)/shard_map/while/body/eval_jaxpr/qa,nab->nqb/dot_general | solution.py:37
  175.3 8.6 %fusion.83 = f32[32,256]{1,0:T(8,128)S(1)} fusion(f32[32,256,256]{1,2,0:T(8,128)S(1)} %fusion.82, bf16[32,256,256]{1,2,0:T(8,128)(2,1)S(1)} %bitcast.127, f32[]{:T(128)} %get-tuple-element.773, f32[]{:T(128)} %get-tuple-element.772, f32[]{:T(128)} %get-tuple-element.771, f32[]{:T(128)} %get-tuple-element.770, f32[]{:T(128)} %get-tuple-element.769, ...), kind=kOutput, calls=%fused_computation.7.clone.1 | convolution fusion | flops 1080090624 | bytes 12621860 | tf_op jit(solution)/shard_map/while/body/eval_jaxpr/nqa,ba->nqb/dot_general | solution.py:38
  195.5 7.3 %fusion.82 = f32[32,256,256]{1,2,0:T(8,128)S(1)} fusion(bf16[32,256,256]{1,2,0:T(8,128)(2,1)S(1)} %bitcast.126, f32[]{:T(128)} %get-tuple-element.764, f32[]{:T(128)} %get-tuple-element.761, f32[]{:T(128)} %get-tuple-element.759, f32[]{:T(128)} %get-tuple-element.757, f32[]{:T(128)} %get-tuple-element.755, f32[]{:T(128)} %get-tuple-element.754, ...), kind=kOutput, calls=%fused_computation.23.clone.1 | convolution fusion | flops 1075904512 | bytes 12589092 | tf_op jit(solution)/shard_map/while/body/eval_jaxpr/qa,nab->nqb/dot_general | solution.py:37
  202.8 8.6 %fusion.83 = f32[32,256]{1,0:T(8,128)S(1)} fusion(f32[32,256,256]{1,2,0:T(8,128)S(1)} %fusion.82, bf16[32,256,256]{1,2,0:T(8,128)(2,1)S(1)} %bitcast.127, f32[]{:T(128)} %get-tuple-element.773, f32[]{:T(128)} %get-tuple-element.772, f32[]{:T(128)} %get-tuple-element.771, f32[]{:T(128)} %get-tuple-element.770, f32[]{:T(128)} %get-tuple-element.769, ...), kind=kOutput, calls=%fused_computation.7.clone.1 | convolution fusion | flops 1080090624 | bytes 12621860 | tf_op jit(solution)/shard_map/while/body/eval_jaxpr/nqa,ba->nqb/dot_general | solution.py:38
  223.0 7.3 %fusion.82 = f32[32,256,256]{1,2,0:T(8,128)S(1)} fusion(bf16[32,256,256]{1,2,0:T(8,128)(2,1)S(1)} %bitcast.126, f32[]{:T(128)} %get-tuple-element.764, f32[]{:T(128)} %get-tuple-element.761, f32[]{:T(128)} %get-tuple-element.759, f32[]{:T(128)} %get-tuple-element.757, f32[]{:T(128)} %get-tuple-element.755, f32[]{:T(128)} %get-tuple-element.754, ...), kind=kOutput, calls=%fused_computation.23.clone.1 | convolution fusion | flops 1075904512 | bytes 12589092 | tf_op jit(solution)/shard_map/while/body/eval_jaxpr/qa,nab->nqb/dot_general | solution.py:37
  230.3 8.6 %fusion.83 = f32[32,256]{1,0:T(8,128)S(1)} fusion(f32[32,256,256]{1,2,0:T(8,128)S(1)} %fusion.82, bf16[32,256,256]{1,2,0:T(8,128)(2,1)S(1)} %bitcast.127, f32[]{:T(128)} %get-tuple-element.773, f32[]{:T(128)} %get-tuple-element.772, f32[]{:T(128)} %get-tuple-element.771, f32[]{:T(128)} %get-tuple-element.770, f32[]{:T(128)} %get-tuple-element.769, ...), kind=kOutput, calls=%fused_computation.7.clone.1 | convolution fusion | flops 1080090624 | bytes 12621860 | tf_op jit(solution)/shard_map/while/body/eval_jaxpr/nqa,ba->nqb/dot_general | solution.py:38
  250.5 7.3 %fusion.82 = f32[32,256,256]{1,2,0:T(8,128)S(1)} fusion(bf16[32,256,256]{1,2,0:T(8,128)(2,1)S(1)} %bitcast.126, f32[]{:T(128)} %get-tuple-element.764, f32[]{:T(128)} %get-tuple-element.761, f32[]{:T(128)} %get-tuple-element.759, f32[]{:T(128)} %get-tuple-element.757, f32[]{:T(128)} %get-tuple-element.755, f32[]{:T(128)} %get-tuple-element.754, ...), kind=kOutput, calls=%fused_computation.23.clone.1 | convolution fusion | flops 1075904512 | bytes 12589092 | tf_op jit(solution)/shard_map/while/body/eval_jaxpr/qa,nab->nqb/dot_general | solution.py:37
  257.9 8.6 %fusion.83 = f32[32,256]{1,0:T(8,128)S(1)} fusion(f32[32,256,256]{1,2,0:T(8,128)S(1)} %fusion.82, bf16[32,256,256]{1,2,0:T(8,128)(2,1)S(1)} %bitcast.127, f32[]{:T(128)} %get-tuple-element.773, f32[]{:T(128)} %get-tuple-element.772, f32[]{:T(128)} %get-tuple-element.771, f32[]{:T(128)} %get-tuple-element.770, f32[]{:T(128)} %get-tuple-element.769, ...), kind=kOutput, calls=%fused_computation.7.clone.1 | convolution fusion | flops 1080090624 | bytes 12621860 | tf_op jit(solution)/shard_map/while/body/eval_jaxpr/nqa,ba->nqb/dot_general | solution.py:38
  278.0 7.3 %fusion.82 = f32[32,256,256]{1,2,0:T(8,128)S(1)} fusion(bf16[32,256,256]{1,2,0:T(8,128)(2,1)S(1)} %bitcast.126, f32[]{:T(128)} %get-tuple-element.764, f32[]{:T(128)} %get-tuple-element.761, f32[]{:T(128)} %get-tuple-element.759, f32[]{:T(128)} %get-tuple-element.757, f32[]{:T(128)} %get-tuple-element.755, f32[]{:T(128)} %get-tuple-element.754, ...), kind=kOutput, calls=%fused_computation.23.clone.1 | convolution fusion | flops 1075904512 | bytes 12589092 | tf_op jit(solution)/shard_map/while/body/eval_jaxpr/qa,nab->nqb/dot_general | solution.py:37
  285.4 8.6 %fusion.83 = f32[32,256]{1,0:T(8,128)S(1)} fusion(f32[32,256,256]{1,2,0:T(8,128)S(1)} %fusion.82, bf16[32,256,256]{1,2,0:T(8,128)(2,1)S(1)} %bitcast.127, f32[]{:T(128)} %get-tuple-element.773, f32[]{:T(128)} %get-tuple-element.772, f32[]{:T(128)} %get-tuple-element.771, f32[]{:T(128)} %get-tuple-element.770, f32[]{:T(128)} %get-tuple-element.769, ...), kind=kOutput, calls=%fused_computation.7.clone.1 | convolution fusion | flops 1080090624 | bytes 12621860 | tf_op jit(solution)/shard_map/while/body/eval_jaxpr/nqa,ba->nqb/dot_general | solution.py:38
  305.6 7.3 %fusion.82 = f32[32,256,256]{1,2,0:T(8,128)S(1)} fusion(bf16[32,256,256]{1,2,0:T(8,128)(2,1)S(1)} %bitcast.126, f32[]{:T(128)} %get-tuple-element.764, f32[]{:T(128)} %get-tuple-element.761, f32[]{:T(128)} %get-tuple-element.759, f32[]{:T(128)} %get-tuple-element.757, f32[]{:T(128)} %get-tuple-element.755, f32[]{:T(128)} %get-tuple-element.754, ...), kind=kOutput, calls=%fused_computation.23.clone.1 | convolution fusion | flops 1075904512 | bytes 12589092 | tf_op jit(solution)/shard_map/while/body/eval_jaxpr/qa,nab->nqb/dot_general | solution.py:37
  312.9 8.6 %fusion.83 = f32[32,256]{1,0:T(8,128)S(1)} fusion(f32[32,256,256]{1,2,0:T(8,128)S(1)} %fusion.82, bf16[32,256,256]{1,2,0:T(8,128)(2,1)S(1)} %bitcast.127, f32[]{:T(128)} %get-tuple-element.773, f32[]{:T(128)} %get-tuple-element.772, f32[]{:T(128)} %get-tuple-element.771, f32[]{:T(128)} %get-tuple-element.770, f32[]{:T(128)} %get-tuple-element.769, ...), kind=kOutput, calls=%fused_computation.7.clone.1 | convolution fusion | flops 1080090624 | bytes 12621860 | tf_op jit(solution)/shard_map/while/body/eval_jaxpr/nqa,ba->nqb/dot_general | solution.py:38
  333.1 7.3 %fusion.82 = f32[32,256,256]{1,2,0:T(8,128)S(1)} fusion(bf16[32,256,256]{1,2,0:T(8,128)(2,1)S(1)} %bitcast.126, f32[]{:T(128)} %get-tuple-element.764, f32[]{:T(128)} %get-tuple-element.761, f32[]{:T(128)} %get-tuple-element.759, f32[]{:T(128)} %get-tuple-element.757, f32[]{:T(128)} %get-tuple-element.755, f32[]{:T(128)} %get-tuple-element.754, ...), kind=kOutput, calls=%fused_computation.23.clone.1 | convolution fusion | flops 1075904512 | bytes 12589092 | tf_op jit(solution)/shard_map/while/body/eval_jaxpr/qa,nab->nqb/dot_general | solution.py:37
  340.4 8.6 %fusion.83 = f32[32,256]{1,0:T(8,128)S(1)} fusion(f32[32,256,256]{1,2,0:T(8,128)S(1)} %fusion.82, bf16[32,256,256]{1,2,0:T(8,128)(2,1)S(1)} %bitcast.127, f32[]{:T(128)} %get-tuple-element.773, f32[]{:T(128)} %get-tuple-element.772, f32[]{:T(128)} %get-tuple-element.771, f32[]{:T(128)} %get-tuple-element.770, f32[]{:T(128)} %get-tuple-element.769, ...), kind=kOutput, calls=%fused_computation.7.clone.1 | convolution fusion | flops 1080090624 | bytes 12621860 | tf_op jit(solution)/shard_map/while/body/eval_jaxpr/nqa,ba->nqb/dot_general | solution.py:38
  349.3 12.5 %all_to_all.22 = f32[32,1,8]{2,1,0:T(1,128)S(1)} all-to-all(f32[32,1,8]{2,1,0:T(1,128)S(1)} %bitcast.132), channel_id=1, replica_groups=mesh['db'=8,'pb'=4] {'db','pb'}, dimensions={0} | all-to-all | bytes 2048 | tf_op jit(solution)/shard_map/all_to_all | solution.py:103
  (110 shorter events, 95.6 us)
Async XLA Ops:
  16.0 14.6 %all-to-all-start = ((s32[2,32,8]{2,0,1:T(2,128)}), s32[2,32,8]{2,0,1:T(2,128)S(1)}, u32[]{:S(2)}, u32[]{:S(2)}) async-start(s32[2,32,8]{2,0,1:T(2,128)} %copy.24), calls=%async_computation | async-start | bytes 65536 | tf_op jit(solution)/shard_map/all_to_all | solution.py:98
  33.1 3.8 %copy-start.1 = (bf16[3,3]{1,0:T(4,128)(2,1)S(1)}, bf16[3,3]{1,0:T(4,128)(2,1)}, u32[]{:S(2)}) copy-start(bf16[3,3]{1,0:T(4,128)(2,1)} %param.10) | copy-start | bytes 58
  33.1 4.5 %copy-start.2 = (bf16[3,3]{1,0:T(4,128)(2,1)S(1)}, bf16[3,3]{1,0:T(4,128)(2,1)}, u32[]{:S(2)}) copy-start(bf16[3,3]{1,0:T(4,128)(2,1)} %param.11) | copy-start | bytes 58
  33.1 95.9 %all-to-all-start.1 = ((bf16[32,1,256,256]{3,2,1,0:T(8,128)(2,1)}), bf16[32,1,256,256]{3,2,1,0:T(8,128)(2,1)}, u32[]{:S(2)}, u32[]{:S(2)}) async-start(bf16[32,1,256,256]{3,2,1,0:T(8,128)(2,1)} %stack.11), calls=%async_computation.1 | async-start | bytes 8388608 | tf_op jit(solution)/shard_map/all_to_all | solution.py:94
  36.8 4.5 %copy-start = (bf16[32,256,256]{2,1,0:T(8,128)(2,1)S(1)}, bf16[32,256,256]{2,1,0:T(8,128)(2,1)}, u32[]{:S(2)}) copy-start(bf16[32,256,256]{2,1,0:T(8,128)(2,1)} %param.8) | copy-start | bytes 12582916
  363.1 2.7 copy-start.3
